TPU v7x, 32 devices: a whole 2x2x4 slice. The times are simulated.
32 devices in a mesh: fsdp: 4 (over z), lat: 8 (over y, x, core).
Axes of the slice: x: 2, y: 2, z: 4, core: 2. Of those that a mesh axis runs over, the one named last changes fastest.
Arguments:
- fields: bfloat16 [4, 128, 360, 192], P('fsdp', 'lat'), may hold values from -6 to 6
- cotangent: bfloat16 [4, 128, 360, 192], P('fsdp', 'lat'), may hold values from -6 to 6
- kernel_one: bfloat16 [3, 3, 192, 192], P(None, None, None, 'fsdp'), may hold values from -0.15625 to 0.15625
- kernel_two: bfloat16 [3, 3, 192, 192], P(None, None, None, 'fsdp'), may hold values from -0.15625 to 0.15625
Outputs:
- block_out: bfloat16 [4, 128, 360, 192], P('fsdp', 'lat')
- field_grad: bfloat16 [4, 128, 360, 192], P('fsdp', 'lat')
- grad_one: float32 [3, 3, 192, 192], P(None, None, None, 'fsdp')
- grad_two: float32 [3, 3, 192, 192], P(None, None, None, 'fsdp')
All inputs are finite; a program needn't handle non-finite values.
Results may differ from a plain program's by a relative error of at most 0.0033.
Values may be sent and summed in bfloat16 or wider, within the bound.
No kernel may reach another device: no remote copies, remote signals or barrier semaphores. Data moves between devices by JAX's collectives and lax.ppermute only.
A program may use at most 128 MiB of HBM per device.

v0:
```python
import jax
import jax.numpy as jnp
from jax import lax
from jax.sharding import PartitionSpec as P


def extended(cells, sides, width):
    for axis, dim in sides:
        count = lax.axis_size(axis)
        ends = count - 1
        head = lax.slice_in_dim(cells, 0, width, axis=dim)
        tail = lax.slice_in_dim(cells, cells.shape[dim] - width, cells.shape[dim], axis=dim)
        cells = jnp.concatenate(
            [
                lax.ppermute(tail, axis, [(i, (i + 1) % count) for i in range(ends)]),
                cells,
                lax.ppermute(head, axis, [((i + 1) % count, i) for i in range(ends)]),
            ],
            axis=dim,
        )
    return cells


def wrap_longitude(values):
    return jnp.concatenate([values[:, :, -2:], values, values[:, :, :2]], axis=2)


def padded_rows(values):
    return wrap_longitude(extended(values, (("lat", 1),), 2))


def correlate(padded, kernel):
    return lax.conv_general_dilated(
        padded,
        kernel,
        (1, 1),
        "VALID",
        rhs_dilation=(2, 2),
        dimension_numbers=("NHWC", "HWIO", "NHWC"),
        preferred_element_type=jnp.float32,
    )


def adjoint_kernel(kernel):
    return jnp.transpose(kernel[::-1, ::-1], (0, 1, 3, 2))


def normal_cdf(values):
    return 0.5 * (1.0 + jax.scipy.special.erf(values * 0.7071067811865476))


def kernel_terms(padded, grad_field, height, width_cells):
    return jnp.stack(
        [
            jnp.stack(
                [
                    jnp.einsum(
                        "nhwc,nhwd->cd",
                        padded[:, 2 * a : 2 * a + height, 2 * b : 2 * b + width_cells],
                        grad_field,
                        preferred_element_type=jnp.float32,
                    )
                    for b in range(3)
                ]
            )
            for a in range(3)
        ]
    )


def per_device(fields, cotangent, kernel_one, kernel_two):
    height = fields.shape[1]
    width_cells = fields.shape[2]
    cell_count = (
        lax.axis_size("fsdp") * fields.shape[0] * lax.axis_size("lat") * height * width_cells
    )
    factor = 1.0 / jnp.sqrt(jnp.float32(cell_count))
    full_one, full_two = (
        lax.all_gather(kernel_one, "fsdp", axis=3, tiled=True),
        lax.all_gather(kernel_two, "fsdp", axis=3, tiled=True),
    )
    source_pad = padded_rows(fields)
    preact = correlate(source_pad, full_one)
    hidden = (preact * normal_cdf(preact)).astype(jnp.bfloat16)
    hidden_pad = padded_rows(hidden)
    block_out = (fields.astype(jnp.float32) + correlate(hidden_pad, full_two)).astype(jnp.bfloat16)
    back = correlate(padded_rows(cotangent), adjoint_kernel(full_two))
    slope = normal_cdf(preact) + preact * jnp.exp(-0.5 * preact * preact) * 0.3989422804014327
    inner_grad = (back * slope).astype(jnp.bfloat16)
    field_grad = (
        cotangent.astype(jnp.float32) + correlate(padded_rows(inner_grad), adjoint_kernel(full_one))
    ).astype(jnp.bfloat16)
    terms_two = kernel_terms(hidden_pad, cotangent, height, width_cells) * factor
    terms_one = kernel_terms(source_pad, inner_grad, height, width_cells) * factor
    share_one, share_two = (
        lax.psum_scatter(terms_one, "fsdp", scatter_dimension=3, tiled=True),
        lax.psum_scatter(terms_two, "fsdp", scatter_dimension=3, tiled=True),
    )
    grad_one, grad_two = lax.psum((share_one, share_two), "lat")
    return (block_out, field_grad, grad_one, grad_two)


def solution(mesh):
    placed = (
        P("fsdp", "lat", None, None),
        P("fsdp", "lat", None, None),
        P(None, None, None, "fsdp"),
        P(None, None, None, "fsdp"),
    )
    return jax.shard_map(
        per_device,
        mesh=mesh,
        in_specs=placed,
        out_specs=(
            P("fsdp", "lat", None, None),
            P("fsdp", "lat", None, None),
            P(None, None, None, "fsdp"),
            P(None, None, None, "fsdp"),
        ),
        check_vma=False,
    )
```

profile of v0, /device:TPU:0, one launch (start us, length us, event | category | flops | bytes accessed | tf_op | source)
XLA Modules:
  0.0 521.3 jit_solution(12465785678488781029)
XLA Ops:
  16.7 5.2 %collective-permute-start.4 = (bf16[1,2,360,192]{2,3,1,0:T(8,128)(2,1)}, bf16[1,2,360,192]{2,3,1,0:T(8,128)(2,1)S(1)}, u32[]{:S(2)}, u32[]{:S(2)}) collective-permute-start(bf16[1,2,360,192]{2,3,1,0:T(8,128)(2,1)} %get-tuple-element.33), channel_id=1, source_target_pairs={{0,1},{1,2},{2,3},{3,4},{4,5},{5,6},{6,7},{8,9},{9,10},{10,11},{11... | collective-permute-start | bytes 829448 | tf_op jit(solution)/shard_map/ppermute | solution.py:15
  21.9 21.1 %all_gather.6 = bf16[3,3,192,192]{2,3,1,0:T(8,128)(2,1)} all-gather(bf16[3,3,192,48]{2,3,1,0:T(8,128)(2,1)} %param.6), channel_id=1, replica_groups=mesh['fsdp'=4,'lat'=8] {'fsdp'}, dimensions={3}, use_global_device_ids=true | all-gather | bytes 829440 | tf_op jit(solution)/shard_map/all_gather | solution.py:79
  43.0 4.9 copy.44
  52.7 20.2 %all_gather.7 = bf16[3,3,192,192]{2,3,1,0:T(8,128)(2,1)} all-gather(bf16[3,3,192,48]{2,3,1,0:T(8,128)(2,1)} %param.7), channel_id=1, replica_groups=mesh['fsdp'=4,'lat'=8] {'fsdp'}, dimensions={3}, use_global_device_ids=true | all-gather | bytes 829440 | tf_op jit(solution)/shard_map/all_gather | solution.py:80
  83.0 11.5 %reshape.194 = bf16[20,1,8,46,192]{3,2,4,0,1:T(8,128)(2,1)} reshape(bf16[20,1,368,192]{2,3,0,1:T(8,128)(2,1)} %pad) | data formatting | bytes 5652480 | tf_op jit(solution)/shard_map/conv_general_dilated | solution.py:33
  94.6 11.8 %copy.47 = bf16[20,1,8,46,192]{4,2,3,0,1:T(8,128)(2,1)} copy(bf16[20,1,8,46,192]{3,2,4,0,1:T(8,128)(2,1)} %reshape.194) | data formatting | bytes 5652480 | tf_op jit(solution)/shard_map/conv_general_dilated | solution.py:33
  107.4 8.6 %reshape.196 = bf16[20,1,8,46,192]{3,2,4,0,1:T(8,128)(2,1)} reshape(bf16[20,1,368,192]{2,3,0,1:T(8,128)(2,1)S(1)} %pad.4) | data formatting | bytes 5652480 | tf_op jit(solution)/shard_map/conv_general_dilated | solution.py:33
  116.0 11.8 %copy.61 = bf16[20,1,8,46,192]{4,2,3,0,1:T(8,128)(2,1)} copy(bf16[20,1,8,46,192]{3,2,4,0,1:T(8,128)(2,1)} %reshape.196) | data formatting | bytes 5652480 | tf_op jit(solution)/shard_map/conv_general_dilated | solution.py:33
  128.9 12.3 %multiply_convert_fusion = (bf16[16,8,46,192]{3,1,2,0:T(8,128)(2,1)}, f32[16,8,46,192]{3,1,2,0:T(8,128)S(1)}) fusion(pred[8,46]{0,1:T(8,128)(4,1)S(1)} %copy-done.35, bf16[3,3,192,192]{2,3,1,0:T(8,128)(2,1)S(1)} %copy-done.20, bf16[20,1,7,4,192]{4,2,3,0,1:T(8,128)(2,1)S(1)} %slice.162, bf16[20,1,8,46,192]{4,2,3,0,1:T(8,128)(2,1)} %copy.47), kind=kOutput, calls=%fused_computation.12 | convolution fusion | flops 3922993152 | bytes 10488176 | tf_op jit(solution)/shard_map/conv_general_dilated | solution.py:33
  141.2 10.5 %fusion.9 = bf16[16,8,46,192]{3,1,2,0:T(8,128)(2,1)S(1)} fusion(f32[16,8,46,192]{3,1,2,0:T(8,128)S(1)} %get-tuple-element.37, pred[8,46]{0,1:T(8,128)(4,1)S(1)} %copy-done.35, bf16[3,3,192,192]{2,3,1,0:T(8,128)(2,1)S(1)} %copy-done.22, bf16[20,1,7,4,192]{4,2,3,0,1:T(8,128)(2,1)S(1)} %slice.172, bf16[20,1,8,46,192]{4,2,3,0,1:T(8,128)(2,1)S(1)} %copy-done.15), kind=kOutput, calls=%fused_computation.11 | convolution fusion | flops 3929776128 | bytes 10488176 | tf_op jit(solution)/shard_map/conv_general_dilated | solution.py:33
  155.7 4.0 copy.98
  159.7 4.5 fusion.191
  190.6 4.7 copy.73
  197.1 3.7 copy.97
  202.7 4.2 collective-permute-start.2
  221.9 4.7 maximum_maximum_fusion
  232.9 5.0 fusion.43
  239.9 3.8 maximum_bitcast_fusion.1
  249.8 4.2 copy.74
  254.0 8.6 %reshape.195 = bf16[20,1,8,46,192]{3,2,4,0,1:T(8,128)(2,1)} reshape(bf16[20,1,368,192]{2,3,0,1:T(8,128)(2,1)S(1)} %copy-done.11) | data formatting | bytes 5652480 | tf_op jit(solution)/shard_map/conv_general_dilated | solution.py:33
  262.6 11.8 %copy.56 = bf16[20,1,8,46,192]{4,2,3,0,1:T(8,128)(2,1)} copy(bf16[20,1,8,46,192]{3,2,4,0,1:T(8,128)(2,1)} %reshape.195) | data formatting | bytes 5652480 | tf_op jit(solution)/shard_map/conv_general_dilated | solution.py:33
  275.7 9.7 %broadcast_select_fusion.1 = f32[16,8,46,192]{3,1,2,0:T(8,128)S(1)} fusion(pred[8,46]{0,1:T(8,128)(4,1)S(1)} %copy-done.35, bf16[3,3,192,192]{2,3,1,0:T(8,128)(2,1)S(1)} %copy-done.23, bf16[20,1,7,4,192]{4,2,3,0,1:T(8,128)(2,1)S(1)} %slice.168, bf16[20,1,8,46,192]{4,2,3,0,1:T(8,128)(2,1)} %copy.56), kind=kOutput, calls=%fused_computation.49 | convolution fusion | flops 3917340672 | bytes 8227184 | tf_op jit(solution)/shard_map/conv_general_dilated | solution.py:33
  285.5 3.5 copy.57
  291.6 4.9 copy.75
  296.5 8.6 %reshape.197 = bf16[20,1,8,46,192]{3,2,4,0,1:T(8,128)(2,1)} reshape(bf16[20,1,368,192]{2,3,0,1:T(8,128)(2,1)S(1)} %copy-done.10) | data formatting | bytes 5652480 | tf_op jit(solution)/shard_map/conv_general_dilated | solution.py:33
  305.0 12.0 %copy.70 = bf16[20,1,8,46,192]{4,2,3,0,1:T(8,128)(2,1)} copy(bf16[20,1,8,46,192]{3,2,4,0,1:T(8,128)(2,1)} %reshape.197) | data formatting | bytes 5652480 | tf_op jit(solution)/shard_map/conv_general_dilated | solution.py:33
  318.2 9.1 %broadcast_select_fusion = f32[16,8,46,192]{3,1,2,0:T(8,128)S(1)} fusion(pred[8,46]{0,1:T(8,128)(4,1)S(1)} %copy-done.35, bf16[3,3,192,192]{2,3,1,0:T(8,128)(2,1)S(1)} %copy-done.21, bf16[20,1,7,4,192]{4,2,3,0,1:T(8,128)(2,1)S(1)} %slice.178, bf16[20,1,8,46,192]{4,2,3,0,1:T(8,128)(2,1)} %copy.70), kind=kOutput, calls=%fused_computation.48 | convolution fusion | flops 3917340672 | bytes 8227184 | tf_op jit(solution)/shard_map/conv_general_dilated | solution.py:33
  327.2 6.1 %copy.71 = f32[16,8,46,192]{3,0,2,1:T(8,128)} copy(f32[16,8,46,192]{3,1,2,0:T(8,128)S(1)} %broadcast_select_fusion) | data formatting | bytes 9043968 | tf_op jit(solution)/shard_map/conv_general_dilated | solution.py:33
  333.3 116.8 %all-reduce.9.cloned.1.call-done = (f32[3,3,192,192]{2,1,0,3:T(4,128)}, f32[3,3,192,192]{2,1,0,3:T(4,128)}) async-done(((f32[3,3,192,192]{2,1,0,3:T(4,128)}, f32[3,3,192,192]{2,1,0,3:T(4,128)}), (f32[3,3,192,192]{2,1,0,3:T(4,128)}, f32[3,3,192,192]{2,1,0,3:T(4,128)})) %all-reduce.9.cloned.1.call-update) | async-done | bytes 2654224
  454.2 5.3 %fusion.11 = bf16[1,16,360,192]{3,1,2,0:T(8,128)(2,1)} fusion(f32[16,1,368,192]{3,0,2,1:T(8,128)} %bitcast.330, bf16[1,16,360,192]{3,1,2,0:T(8,128)(2,1)S(1)} %copy-done.8), kind=kLoop, calls=%fused_computation.16 | loop fusion | flops 3317760 | bytes 8847360 | tf_op jit(solution)/shard_map/convert_element_type | solution.py:92
  459.5 4.7 copy.76
  464.2 46.3 %all-reduce.7.cloned.1.call-done = (f32[3,3,192,48]{2,1,0,3:T(4,128)}, f32[3,3,192,48]{2,1,0,3:T(4,128)}) async-done(((f32[3,3,192,48]{2,1,0,3:T(4,128)}, f32[3,3,192,48]{2,1,0,3:T(4,128)}), (f32[3,3,192,48]{2,1,0,3:T(4,128)}, f32[3,3,192,48]{2,1,0,3:T(4,128)})) %all-reduce.7.cloned.1.call-update) | async-done | bytes 663568 | tf_op jit(solution)/shard_map/psum | solution.py:99
  (159 shorter events, 101.5 us)
Async XLA Ops:
  7.2 443.0 %all-reduce.9.cloned.1.call-start = ((), (), s32[]{:S(2)}) async-start(), calls=%async_computation.1 | async-start | bytes 9437184
  9.1 66.7 %collective-permute-start.1 = (bf16[1,2,360,192]{2,3,1,0:T(8,128)(2,1)}, bf16[1,2,360,192]{2,3,1,0:T(8,128)(2,1)S(1)}, u32[]{:S(2)}, u32[]{:S(2)}) collective-permute-start(bf16[1,2,360,192]{2,3,1,0:T(8,128)(2,1)} %get-tuple-element.34), channel_id=1, source_target_pairs={{1,0},{2,1},{3,2},{4,3},{5,4},{6,5},{7,6},{9,8},{10,9},{11,10},{12... | collective-permute-start | bytes 829448 | tf_op jit(solution)/shard_map/ppermute | solution.py:17
  10.4 63.1 %collective-permute-start = (bf16[1,2,360,192]{2,3,1,0:T(8,128)(2,1)}, bf16[1,2,360,192]{2,3,1,0:T(8,128)(2,1)S(1)}, u32[]{:S(2)}, u32[]{:S(2)}) collective-permute-start(bf16[1,2,360,192]{2,3,1,0:T(8,128)(2,1)} %get-tuple-element.35), channel_id=1, source_target_pairs={{0,1},{1,2},{2,3},{3,4},{4,5},{5,6},{6,7},{8,9},{9,10},{10,11},{11... | collective-permute-start | bytes 829448 | tf_op jit(solution)/shard_map/ppermute | solution.py:15
  15.4 59.8 %collective-permute-start.5 = (bf16[1,2,360,192]{2,3,1,0:T(8,128)(2,1)}, bf16[1,2,360,192]{2,3,1,0:T(8,128)(2,1)S(1)}, u32[]{:S(2)}, u32[]{:S(2)}) collective-permute-start(bf16[1,2,360,192]{2,3,1,0:T(8,128)(2,1)} %get-tuple-element.32), channel_id=1, source_target_pairs={{1,0},{2,1},{3,2},{4,3},{5,4},{6,5},{7,6},{9,8},{10,9},{11,10},{12... | collective-permute-start | bytes 829448 | tf_op jit(solution)/shard_map/ppermute | solution.py:17
  16.7 31.3 %copy-start.2 = (bf16[1,16,360,192]{2,3,1,0:T(8,128)(2,1)S(1)}, bf16[1,16,360,192]{2,3,1,0:T(8,128)(2,1)}, u32[]{:S(2)}) copy-start(bf16[1,16,360,192]{2,3,1,0:T(8,128)(2,1)} %param.5) | copy-start | bytes 6635524
  16.7 56.3 %collective-permute-start.4 = (bf16[1,2,360,192]{2,3,1,0:T(8,128)(2,1)}, bf16[1,2,360,192]{2,3,1,0:T(8,128)(2,1)S(1)}, u32[]{:S(2)}, u32[]{:S(2)}) collective-permute-start(bf16[1,2,360,192]{2,3,1,0:T(8,128)(2,1)} %get-tuple-element.33), channel_id=1, source_target_pairs={{0,1},{1,2},{2,3},{3,4},{4,5},{5,6},{6,7},{8,9},{9,10},{10,11},{11... | collective-permute-start | bytes 829448 | tf_op jit(solution)/shard_map/ppermute | solution.py:15
  47.9 3.5 copy-start.34
  75.9 3.1 copy-start.12
  116.0 12.9 %copy-start.20 = (bf16[3,3,192,192]{2,3,1,0:T(8,128)(2,1)S(1)}, bf16[3,3,192,192]{2,3,1,0:T(8,128)(2,1)}, u32[]{:S(2)}) copy-start(bf16[3,3,192,192]{2,3,1,0:T(8,128)(2,1)} %all_gather.6) | copy-start | bytes 1990660
  116.0 12.9 %copy-start.35 = (pred[8,46]{0,1:T(8,128)(4,1)S(1)}, pred[8,46]{0,1:T(8,128)(4,1)}, u32[]{:S(2)}) copy-start(pred[8,46]{0,1:T(8,128)(4,1)} %constant.30) | copy-start | bytes 1108
  128.9 12.4 %copy-start.15 = (bf16[20,1,8,46,192]{4,2,3,0,1:T(8,128)(2,1)S(1)}, bf16[20,1,8,46,192]{4,2,3,0,1:T(8,128)(2,1)}, u32[]{:S(2)}) copy-start(bf16[20,1,8,46,192]{4,2,3,0,1:T(8,128)(2,1)} %copy.61) | copy-start | bytes 8478724
  128.9 12.3 %copy-start.22 = (bf16[3,3,192,192]{2,3,1,0:T(8,128)(2,1)S(1)}, bf16[3,3,192,192]{2,3,1,0:T(8,128)(2,1)}, u32[]{:S(2)}) copy-start(bf16[3,3,192,192]{2,3,1,0:T(8,128)(2,1)} %all_gather.7) | copy-start | bytes 1990660
  155.6 4.0 copy-start.19
  159.7 28.1 %copy-start = (bf16[16,1,360,192]{2,3,0,1:T(8,128)(2,1)}, bf16[16,1,360,192]{2,3,0,1:T(8,128)(2,1)S(1)}, u32[]{:S(2)}) copy-start(bf16[16,1,360,192]{2,3,0,1:T(8,128)(2,1)S(1)} %copy.98) | copy-start | bytes 6635524
  159.7 4.5 copy-start.13
  159.7 4.5 copy-start.17
  182.9 4.8 copy-start.32
  182.9 4.8 copy-start.33
  182.9 4.9 copy-start.6
  182.9 4.9 copy-start.26
  182.9 49.4 %collective-permute-start.6 = (bf16[1,2,360,192]{2,3,1,0:T(8,128)(2,1)}, bf16[1,2,360,192]{2,3,1,0:T(8,128)(2,1)}, u32[]{:S(2)}, u32[]{:S(2)}) collective-permute-start(bf16[1,2,360,192]{2,3,1,0:T(8,128)(2,1)} %slice_bitcast_fusion.27), channel_id=1, source_target_pairs={{0,1},{1,2},{2,3},{3,4},{4,5},{5,6},{6,7},{8,9},{9,10},{10,11},{11... | collective-permute-start | bytes 829448 | tf_op jit(solution)/shard_map/ppermute | solution.py:15
  190.6 4.7 copy-start.7
  202.7 17.7 %collective-permute-start.2 = (bf16[1,2,360,192]{2,3,1,0:T(8,128)(2,1)}, bf16[1,2,360,192]{2,3,1,0:T(8,128)(2,1)S(1)}, u32[]{:S(2)}, u32[]{:S(2)}) collective-permute-start(bf16[1,2,360,192]{2,3,1,0:T(8,128)(2,1)} %slice_bitcast_fusion.29), channel_id=1, source_target_pairs={{0,1},{1,2},{2,3},{3,4},{4,5},{5,6},{6,7},{8,9},{9,10},{10,11},{11... | collective-permute-start | bytes 829448 | tf_op jit(solution)/shard_map/ppermute | solution.py:15
  211.5 8.9 %collective-permute-start.3 = (bf16[1,2,360,192]{2,3,1,0:T(8,128)(2,1)}, bf16[1,2,360,192]{2,3,1,0:T(8,128)(2,1)}, u32[]{:S(2)}, u32[]{:S(2)}) collective-permute-start(bf16[1,2,360,192]{2,3,1,0:T(8,128)(2,1)} %slice_bitcast_fusion.28), channel_id=1, source_target_pairs={{1,0},{2,1},{3,2},{4,3},{5,4},{6,5},{7,6},{9,8},{10,9},{11,10},{12... | collective-permute-start | bytes 829448 | tf_op jit(solution)/shard_map/ppermute | solution.py:17
  216.7 15.7 %collective-permute-start.7 = (bf16[1,2,360,192]{2,3,1,0:T(8,128)(2,1)S(1)}, bf16[1,2,360,192]{2,3,1,0:T(8,128)(2,1)S(1)}, u32[]{:S(2)}, u32[]{:S(2)}) collective-permute-start(bf16[1,2,360,192]{2,3,1,0:T(8,128)(2,1)S(1)} %slice_bitcast_fusion.26), channel_id=1, source_target_pairs={{1,0},{2,1},{3,2},{4,3},{5,4},{6,5},{7,6},{9,8},{10,9},{11,10},{12... | collective-permute-start | bytes 829448 | tf_op jit(solution)/shard_map/ppermute | solution.py:17
  221.9 4.7 copy-start.3
  249.8 4.2 copy-start.11
  275.5 235.0 %all-reduce.7.cloned.1.call-start = ((), (), s32[]{:S(2)}) async-start(), calls=%async_computation | async-start | bytes 2359296 | tf_op jit(solution)/shard_map/psum | solution.py:99
  285.5 3.5 copy-start.9
  291.6 4.9 copy-start.10
  305.0 13.1 %copy-start.21 = (bf16[3,3,192,192]{2,3,1,0:T(8,128)(2,1)S(1)}, bf16[3,3,192,192]{2,3,1,0:T(8,128)(2,1)}, u32[]{:S(2)}) copy-start(bf16[3,3,192,192]{2,3,1,0:T(8,128)(2,1)} %all_gather.6) | copy-start | bytes 1990660
  333.3 120.8 %copy-start.8 = (bf16[1,16,360,192]{3,1,2,0:T(8,128)(2,1)S(1)}, bf16[1,16,360,192]{3,1,2,0:T(8,128)(2,1)}, u32[]{:S(2)}) copy-start(bf16[1,16,360,192]{3,1,2,0:T(8,128)(2,1)} %copy.58) | copy-start | bytes 6635524
  (14 other events, 21.7 us)
Sparse Core Ops, SparseCore 0:
  275.6 174.4 all-reduce.8
  454.3 56.1 all-reduce.6
where the time goes:
time: 531 us; the launch traced here: 521 us
  local copies, waits for them, and re-layouts  180 us (34%)
  waiting for transfers between devices  163 us (31%)
  matrix products  70.8 us (13%)
  blocking collectives  41.3 us (8%)
  other arithmetic  30 us (6%)
  starting transfers between devices  20.2 us (4%)
  between operations  15.7 us (3%)
    unnamed x3, waiting for transfers between devices  117 us
    conv_general_dilated x14, local copies, waits for them, and re-layouts, correlate(): lax.conv_general_dilated(padded, kernel, (1, 1), 'VALID', rhs_dilation=(2...  98.5 us
    psum x1, waiting for transfers between devices, per_device(): grad_one, grad_two = lax.psum((share_one, share_two), 'lat')  46.3 us
    conv_general_dilated x4, matrix products, correlate(): lax.conv_general_dilated(padded, kernel, (1, 1), 'VALID', rhs_dilation=(2...  41.6 us
    unnamed x87, local copies, waits for them, and re-layouts  37.6 us
    dot_general x18, matrix products, kernel_terms(): jnp.einsum('nhwc,nhwd->cd', padded[:, 2 * a:2 * a + height, 2 * b:2 * b +...  29.2 us
    all_gather x1, blocking collectives, per_device(): lax.all_gather(kernel_one, 'fsdp', axis=3, tiled=True)  21.1 us
    all_gather x1, blocking collectives, per_device(): lax.all_gather(kernel_two, 'fsdp', axis=3, tiled=True)  20.2 us
  transfers between devices with their start and end apart: 10, of which 2 were waited for; matrix products, arithmetic and copies ran while one was open for 23% of the time, Pallas kernels for 0%

commit v1 on v0

--- a/solution.py
+++ b/solution.py
@@ -2,6 +2,11 @@
 import jax.numpy as jnp
 from jax import lax
 from jax.sharding import PartitionSpec as P
+
+
+def all_by_exchange(x, axis, dim):
+    outgoing = jnp.stack([x] * lax.axis_size(axis))
+    return jnp.concatenate(lax.all_to_all(outgoing, axis, 0, 0), axis=dim)
 
 
 def extended(cells, sides, width):
@@ -77,7 +82,7 @@
     factor = 1.0 / jnp.sqrt(jnp.float32(cell_count))
     full_one, full_two = (
         lax.all_gather(kernel_one, "fsdp", axis=3, tiled=True),
-        lax.all_gather(kernel_two, "fsdp", axis=3, tiled=True),
+        all_by_exchange(kernel_two, "fsdp", 3),
     )
     source_pad = padded_rows(fields)
     preact = correlate(source_pad, full_one)

time: 531 us -> 519 us (0.977)
  blocking collectives: 41.3 us -> 27.7 us
  starting transfers between devices: 20.2 us -> 28.4 us
    all_gather x1 -> x0, blocking collectives: 20.2 us -> none  [per_device(): lax.all_gather(kernel_two, 'fsdp', axis=3, tiled=True)]
    all_gather x1, blocking collectives: 21.1 us -> 27.7 us  [per_device(): lax.all_gather(kernel_one, 'fsdp', axis=3, tiled=True)]
    unnamed x87 -> x77, local copies, waits for them, and re-layouts: 37.6 us -> 38.9 us
  transfers between devices with their start and end apart: 10 -> 11, of which waited for: 2 -> 3; matrix products, arithmetic and copies ran while one was open for 23% -> 46% of each run, Pallas kernels for 0% -> 0%
where the time goes in v1:
time: 519 us; the launch traced here: 512 us
  local copies, waits for them, and re-layouts  183 us (35%)
  waiting for transfers between devices  159 us (31%)
  matrix products  71.1 us (14%)
  starting transfers between devices  28.4 us (5%)
  blocking collectives  27.7 us (5%)
  other arithmetic  27.1 us (5%)
  between operations  15.6 us (3%)
    unnamed x3, waiting for transfers between devices  112 us
    conv_general_dilated x14, local copies, waits for them, and re-layouts, correlate(): lax.conv_general_dilated(padded, kernel, (1, 1), 'VALID', rhs_dilation=(2...  103 us
    psum x1, waiting for transfers between devices, per_device(): grad_one, grad_two = lax.psum((share_one, share_two), 'lat')  46.3 us
    conv_general_dilated x4, matrix products, correlate(): lax.conv_general_dilated(padded, kernel, (1, 1), 'VALID', rhs_dilation=(2...  43.7 us
    unnamed x77, local copies, waits for them, and re-layouts  38.9 us
    all_gather x1, blocking collectives, per_device(): lax.all_gather(kernel_one, 'fsdp', axis=3, tiled=True)  27.7 us
    dot_general x18, matrix products, kernel_terms(): jnp.einsum('nhwc,nhwd->cd', padded[:, 2 * a:2 * a + height, 2 * b:2 * b +...  27.5 us
    ppermute x4, starting transfers between devices, extended(): lax.ppermute(tail, axis, [(i, (i + 1) % count) for i in range(ends)])  18.1 us
  transfers between devices with their start and end apart: 11, of which 3 were waited for; matrix products, arithmetic and copies ran while one was open for 46% of the time, Pallas kernels for 0%

profile of v1, /device:TPU:0, one launch (start us, length us, event | category | flops | bytes accessed | tf_op | source)
XLA Modules:
  0.0 512.0 jit_solution(16531133403128375211)
XLA Ops:
  16.7 5.8 %collective-permute-start.4 = (bf16[1,2,360,192]{2,3,1,0:T(8,128)(2,1)}, bf16[1,2,360,192]{2,3,1,0:T(8,128)(2,1)}, u32[]{:S(2)}, u32[]{:S(2)}) collective-permute-start(bf16[1,2,360,192]{2,3,1,0:T(8,128)(2,1)} %get-tuple-element.33), channel_id=1, source_target_pairs={{0,1},{1,2},{2,3},{3,4},{4,5},{5,6},{6,7},{8,9},{9,10},{10,11},{11... | collective-permute-start | bytes 829448 | tf_op jit(solution)/shard_map/ppermute | solution.py:20
  24.4 4.9 all-to-all-start
  29.3 5.0 copy.45
  34.3 3.6 copy.60
  39.1 27.7 %all_gather.3 = bf16[3,3,192,192]{2,3,1,0:T(8,128)(2,1)S(1)} all-gather(bf16[3,3,192,48]{2,3,1,0:T(8,128)(2,1)} %param.6), channel_id=1, replica_groups=mesh['fsdp'=4,'lat'=8] {'fsdp'}, dimensions={3}, use_global_device_ids=true | all-gather | bytes 829440 | tf_op jit(solution)/shard_map/all_gather | solution.py:84
  75.1 11.7 %reshape.204 = bf16[20,1,8,46,192]{3,2,4,0,1:T(8,128)(2,1)} reshape(bf16[20,1,368,192]{2,3,0,1:T(8,128)(2,1)} %pad) | data formatting | bytes 5652480 | tf_op jit(solution)/shard_map/conv_general_dilated | solution.py:38
  86.8 11.8 %copy.48 = bf16[20,1,8,46,192]{4,2,3,0,1:T(8,128)(2,1)} copy(bf16[20,1,8,46,192]{3,2,4,0,1:T(8,128)(2,1)} %reshape.204) | data formatting | bytes 5652480 | tf_op jit(solution)/shard_map/conv_general_dilated | solution.py:38
  99.7 12.0 %multiply_convert_fusion = (bf16[16,8,46,192]{3,1,2,0:T(8,128)(2,1)S(1)}, f32[16,8,46,192]{3,1,2,0:T(8,128)}) fusion(pred[8,46]{0,1:T(8,128)(4,1)S(1)} %copy-done.30, bf16[3,3,192,192]{2,3,1,0:T(8,128)(2,1)S(1)} %all_gather.3, bf16[20,1,7,4,192]{4,2,3,0,1:T(8,128)(2,1)S(1)} %slice.162, bf16[20,1,8,46,192]{4,2,3,0,1:T(8,128)(2,1)} %copy.48), kind=kOutput, calls=%fused_computation.12 | convolution fusion | flops 3922993152 | bytes 10488176 | tf_op jit(solution)/shard_map/conv_general_dilated | solution.py:38
  120.4 11.3 %reshape.206 = bf16[20,1,8,46,192]{3,2,4,0,1:T(8,128)(2,1)} reshape(bf16[20,1,368,192]{2,3,0,1:T(8,128)(2,1)} %pad.4) | data formatting | bytes 5652480 | tf_op jit(solution)/shard_map/conv_general_dilated | solution.py:38
  131.7 11.9 %copy.63 = bf16[20,1,8,46,192]{4,2,3,0,1:T(8,128)(2,1)} copy(bf16[20,1,8,46,192]{3,2,4,0,1:T(8,128)(2,1)} %reshape.206) | data formatting | bytes 5652480 | tf_op jit(solution)/shard_map/conv_general_dilated | solution.py:38
  147.1 3.7 copy.99
  163.0 3.7 maximum_maximum_fusion
  180.4 4.2 copy.76
  184.6 8.5 %reshape.205 = bf16[20,1,8,46,192]{3,2,4,0,1:T(8,128)(2,1)} reshape(bf16[20,1,368,192]{2,3,0,1:T(8,128)(2,1)S(1)} %copy-done.6) | data formatting | bytes 5652480 | tf_op jit(solution)/shard_map/conv_general_dilated | solution.py:38
  193.1 11.8 %copy.57 = bf16[20,1,8,46,192]{4,2,3,0,1:T(8,128)(2,1)} copy(bf16[20,1,8,46,192]{3,2,4,0,1:T(8,128)(2,1)} %reshape.205) | data formatting | bytes 5652480 | tf_op jit(solution)/shard_map/conv_general_dilated | solution.py:38
  208.0 12.5 %fusion.9 = bf16[16,8,46,192]{3,1,2,0:T(8,128)(2,1)S(1)} fusion(f32[16,8,46,192]{3,1,2,0:T(8,128)} %get-tuple-element.37, pred[8,46]{0,1:T(8,128)(4,1)S(1)} %copy-done.30, bf16[3,3,192,192]{2,3,1,0:T(8,128)(2,1)S(1)} %bitcast.337, bf16[20,1,7,4,192]{4,2,3,0,1:T(8,128)(2,1)S(1)} %copy-done.20, bf16[20,1,8,46,192]{4,2,3,0,1:T(8,128)(2,1)} %copy.63), kind=kOutput, calls=%fused_computation.11 | convolution fusion | flops 3929776128 | bytes 10488176 | tf_op jit(solution)/shard_map/conv_general_dilated | solution.py:38
  224.3 4.2 copy.100
  228.6 3.7 fusion.191
  245.0 7.9 %collective-permute-start.6 = (bf16[1,2,360,192]{2,3,1,0:T(8,128)(2,1)}, bf16[1,2,360,192]{2,3,1,0:T(8,128)(2,1)}, u32[]{:S(2)}, u32[]{:S(2)}) collective-permute-start(bf16[1,2,360,192]{2,3,1,0:T(8,128)(2,1)} %slice_bitcast_fusion.27), channel_id=1, source_target_pairs={{0,1},{1,2},{2,3},{3,4},{4,5},{5,6},{6,7},{8,9},{9,10},{10,11},{11... | collective-permute-start | bytes 829448 | tf_op jit(solution)/shard_map/ppermute | solution.py:20
  258.3 4.1 copy.75
  266.0 10.2 %broadcast_select_fusion.1 = f32[16,8,46,192]{3,1,2,0:T(8,128)S(1)} fusion(pred[8,46]{0,1:T(8,128)(4,1)S(1)} %copy-done.30, bf16[3,3,192,192]{2,3,1,0:T(8,128)(2,1)S(1)} %bitcast.338, bf16[20,1,7,4,192]{4,2,3,0,1:T(8,128)(2,1)} %slice.168, bf16[20,1,8,46,192]{4,2,3,0,1:T(8,128)(2,1)} %copy.57), kind=kOutput, calls=%fused_computation.49 | convolution fusion | flops 3917340672 | bytes 8227184 | tf_op jit(solution)/shard_map/conv_general_dilated | solution.py:38
  276.2 3.5 copy.59
  282.3 4.7 copy.77
  287.0 5.0 fusion.43
  292.4 8.6 %reshape.207 = bf16[20,1,8,46,192]{3,2,4,0,1:T(8,128)(2,1)} reshape(bf16[20,1,368,192]{2,3,0,1:T(8,128)(2,1)S(1)} %pad.6) | data formatting | bytes 5652480 | tf_op jit(solution)/shard_map/conv_general_dilated | solution.py:38
  301.0 12.1 %copy.72 = bf16[20,1,8,46,192]{4,2,3,0,1:T(8,128)(2,1)} copy(bf16[20,1,8,46,192]{3,2,4,0,1:T(8,128)(2,1)} %reshape.207) | data formatting | bytes 5652480 | tf_op jit(solution)/shard_map/conv_general_dilated | solution.py:38
  314.1 9.1 %broadcast_select_fusion = f32[16,8,46,192]{3,1,2,0:T(8,128)S(1)} fusion(pred[8,46]{0,1:T(8,128)(4,1)S(1)} %copy-done.30, bf16[3,3,192,192]{2,3,1,0:T(8,128)(2,1)S(1)} %copy-done.18, bf16[20,1,7,4,192]{4,2,3,0,1:T(8,128)(2,1)S(1)} %slice.178, bf16[20,1,8,46,192]{4,2,3,0,1:T(8,128)(2,1)} %copy.72), kind=kOutput, calls=%fused_computation.48 | convolution fusion | flops 3917340672 | bytes 8227184 | tf_op jit(solution)/shard_map/conv_general_dilated | solution.py:38
  323.2 6.1 %copy.73 = f32[16,8,46,192]{3,0,2,1:T(8,128)} copy(f32[16,8,46,192]{3,1,2,0:T(8,128)S(1)} %broadcast_select_fusion) | data formatting | bytes 9043968 | tf_op jit(solution)/shard_map/conv_general_dilated | solution.py:38
  329.2 111.6 %all-reduce.9.cloned.1.call-done = (f32[3,3,192,192]{2,1,0,3:T(4,128)}, f32[3,3,192,192]{2,1,0,3:T(4,128)}) async-done(((f32[3,3,192,192]{2,1,0,3:T(4,128)}, f32[3,3,192,192]{2,1,0,3:T(4,128)}), (f32[3,3,192,192]{2,1,0,3:T(4,128)}, f32[3,3,192,192]{2,1,0,3:T(4,128)})) %all-reduce.9.cloned.1.call-update) | async-done | bytes 2654224
  444.8 5.4 %fusion.11 = bf16[1,16,360,192]{3,1,2,0:T(8,128)(2,1)} fusion(f32[16,1,368,192]{3,0,2,1:T(8,128)} %bitcast.333, bf16[1,16,360,192]{3,1,2,0:T(8,128)(2,1)S(1)} %copy-done.4), kind=kLoop, calls=%fused_computation.16 | loop fusion | flops 3317760 | bytes 8847360 | tf_op jit(solution)/shard_map/convert_element_type | solution.py:97
  450.2 4.7 copy.78
  454.9 46.3 %all-reduce.7.cloned.1.call-done = (f32[3,3,192,48]{2,1,0,3:T(4,128)}, f32[3,3,192,48]{2,1,0,3:T(4,128)}) async-done(((f32[3,3,192,48]{2,1,0,3:T(4,128)}, f32[3,3,192,48]{2,1,0,3:T(4,128)}), (f32[3,3,192,48]{2,1,0,3:T(4,128)}, f32[3,3,192,48]{2,1,0,3:T(4,128)})) %all-reduce.7.cloned.1.call-update) | async-done | bytes 663568 | tf_op jit(solution)/shard_map/psum | solution.py:104
  (152 shorter events, 99.3 us)
Async XLA Ops:
  9.1 60.3 %collective-permute-start.1 = (bf16[1,2,360,192]{2,3,1,0:T(8,128)(2,1)}, bf16[1,2,360,192]{2,3,1,0:T(8,128)(2,1)}, u32[]{:S(2)}, u32[]{:S(2)}) collective-permute-start(bf16[1,2,360,192]{2,3,1,0:T(8,128)(2,1)} %get-tuple-element.34), channel_id=1, source_target_pairs={{1,0},{2,1},{3,2},{4,3},{5,4},{6,5},{7,6},{9,8},{10,9},{11,10},{12... | collective-permute-start | bytes 829448 | tf_op jit(solution)/shard_map/ppermute | solution.py:22
  10.4 56.5 %collective-permute-start = (bf16[1,2,360,192]{2,3,1,0:T(8,128)(2,1)}, bf16[1,2,360,192]{2,3,1,0:T(8,128)(2,1)S(1)}, u32[]{:S(2)}, u32[]{:S(2)}) collective-permute-start(bf16[1,2,360,192]{2,3,1,0:T(8,128)(2,1)} %get-tuple-element.35), channel_id=1, source_target_pairs={{0,1},{1,2},{2,3},{3,4},{4,5},{5,6},{6,7},{8,9},{9,10},{10,11},{11... | collective-permute-start | bytes 829448 | tf_op jit(solution)/shard_map/ppermute | solution.py:20
  15.4 99.6 %collective-permute-start.5 = (bf16[1,2,360,192]{2,3,1,0:T(8,128)(2,1)}, bf16[1,2,360,192]{2,3,1,0:T(8,128)(2,1)}, u32[]{:S(2)}, u32[]{:S(2)}) collective-permute-start(bf16[1,2,360,192]{2,3,1,0:T(8,128)(2,1)} %get-tuple-element.32), channel_id=1, source_target_pairs={{1,0},{2,1},{3,2},{4,3},{5,4},{6,5},{7,6},{9,8},{10,9},{11,10},{12... | collective-permute-start | bytes 829448 | tf_op jit(solution)/shard_map/ppermute | solution.py:22
  16.7 95.0 %collective-permute-start.4 = (bf16[1,2,360,192]{2,3,1,0:T(8,128)(2,1)}, bf16[1,2,360,192]{2,3,1,0:T(8,128)(2,1)}, u32[]{:S(2)}, u32[]{:S(2)}) collective-permute-start(bf16[1,2,360,192]{2,3,1,0:T(8,128)(2,1)} %get-tuple-element.33), channel_id=1, source_target_pairs={{0,1},{1,2},{2,3},{3,4},{4,5},{5,6},{6,7},{8,9},{9,10},{10,11},{11... | collective-permute-start | bytes 829448 | tf_op jit(solution)/shard_map/ppermute | solution.py:20
  24.4 182.4 %all-to-all-start = ((bf16[4,3,3,192,48]{3,4,2,1,0:T(8,128)(2,1)}), bf16[4,3,3,192,48]{3,4,2,1,0:T(8,128)(2,1)}, u32[]{:S(2)}, u32[]{:S(2)}) async-start(bf16[4,3,3,192,48]{3,4,2,1,0:T(8,128)(2,1)} %stack.103), calls=%async_computation | async-start | bytes 1769472 | tf_op jit(solution)/shard_map/all_to_all | solution.py:9
  29.3 5.1 copy-start
  29.3 411.5 %all-reduce.9.cloned.1.call-start = ((), (), s32[]{:S(2)}) async-start(), calls=%async_computation.2 | async-start | bytes 9437184
  34.3 3.6 copy-start.29
  66.8 32.8 %copy-start.17 = (bf16[3,3,192,192]{2,3,1,0:T(8,128)(2,1)}, bf16[3,3,192,192]{2,3,1,0:T(8,128)(2,1)S(1)}, u32[]{:S(2)}) copy-start(bf16[3,3,192,192]{2,3,1,0:T(8,128)(2,1)S(1)} %all_gather.3) | copy-start | bytes 1990660
  66.8 3.6 copy-start.21
  70.5 2.5 copy-start.7
  86.8 12.9 %copy-start.30 = (pred[8,46]{0,1:T(8,128)(4,1)S(1)}, pred[8,46]{0,1:T(8,128)(4,1)}, u32[]{:S(2)}) copy-start(pred[8,46]{0,1:T(8,128)(4,1)} %constant.30) | copy-start | bytes 1108
  152.8 8.9 %collective-permute-start.2 = (bf16[1,2,360,192]{2,3,1,0:T(8,128)(2,1)}, bf16[1,2,360,192]{2,3,1,0:T(8,128)(2,1)S(1)}, u32[]{:S(2)}, u32[]{:S(2)}) collective-permute-start(bf16[1,2,360,192]{2,3,1,0:T(8,128)(2,1)} %slice_bitcast_fusion.29), channel_id=1, source_target_pairs={{0,1},{1,2},{2,3},{3,4},{4,5},{5,6},{6,7},{8,9},{9,10},{10,11},{11... | collective-permute-start | bytes 829448 | tf_op jit(solution)/shard_map/ppermute | solution.py:20
  157.9 4.5 collective-permute-start.3
  163.0 3.7 copy-start.1
  179.0 5.6 %copy-start.6 = (bf16[20,1,368,192]{2,3,0,1:T(8,128)(2,1)S(1)}, bf16[20,1,368,192]{2,3,0,1:T(8,128)(2,1)}, u32[]{:S(2)}) copy-start(bf16[20,1,368,192]{2,3,0,1:T(8,128)(2,1)} %pad.2) | copy-start | bytes 8478724
  193.1 14.9 %copy-start.20 = (bf16[20,1,7,4,192]{4,2,3,0,1:T(8,128)(2,1)S(1)}, bf16[20,1,7,4,192]{4,2,3,0,1:T(8,128)(2,1)}, u32[]{:S(2)}) copy-start(bf16[20,1,7,4,192]{4,2,3,0,1:T(8,128)(2,1)} %slice.172) | copy-start | bytes 645124
  208.0 12.5 %copy-start.15 = (bf16[4,3,3,192,48]{3,4,0,2,1:T(8,128)(2,1)}, bf16[4,3,3,192,48]{3,4,0,2,1:T(8,128)(2,1)S(1)}, u32[]{:S(2)}) copy-start(bf16[4,3,3,192,48]{3,4,0,2,1:T(8,128)(2,1)S(1)} %copy.58) | copy-start | bytes 1990660
  224.3 4.2 copy-start.12
  228.6 3.7 copy-start.8
  228.6 3.7 copy-start.10
  244.9 10.5 %copy-start.27 = (f32[1,192,192]{2,1,0:T(8,128)S(1)}, f32[1,192,192]{2,1,0:T(8,128)}, u32[]{:S(2)}) copy-start(f32[1,192,192]{2,1,0:T(8,128)} %fusion.166) | copy-start | bytes 442372
  244.9 10.5 %copy-start.28 = (f32[1,192,192]{2,1,0:T(8,128)S(1)}, f32[1,192,192]{2,1,0:T(8,128)}, u32[]{:S(2)}) copy-start(f32[1,192,192]{2,1,0:T(8,128)} %fusion.156) | copy-start | bytes 442372
  244.9 10.5 %copy-start.3 = (bf16[1,16,360,192]{2,3,1,0:T(8,128)(2,1)S(1)}, bf16[1,16,360,192]{2,3,1,0:T(8,128)(2,1)}, u32[]{:S(2)}) copy-start(bf16[1,16,360,192]{2,3,1,0:T(8,128)(2,1)} %param.4) | copy-start | bytes 6635524
  244.9 10.5 %copy-start.22 = (bf16[1,2,360,192]{2,3,1,0:T(8,128)(2,1)S(1)}, bf16[1,2,360,192]{2,3,1,0:T(8,128)(2,1)}, u32[]{:S(2)}) copy-start(bf16[1,2,360,192]{2,3,1,0:T(8,128)(2,1)} %copy-done.21) | copy-start | bytes 829444
  245.0 42.1 %collective-permute-start.6 = (bf16[1,2,360,192]{2,3,1,0:T(8,128)(2,1)}, bf16[1,2,360,192]{2,3,1,0:T(8,128)(2,1)}, u32[]{:S(2)}, u32[]{:S(2)}) collective-permute-start(bf16[1,2,360,192]{2,3,1,0:T(8,128)(2,1)} %slice_bitcast_fusion.27), channel_id=1, source_target_pairs={{0,1},{1,2},{2,3},{3,4},{4,5},{5,6},{6,7},{8,9},{9,10},{10,11},{11... | collective-permute-start | bytes 829448 | tf_op jit(solution)/shard_map/ppermute | solution.py:20
  258.3 4.1 copy-start.13
  264.3 22.7 %collective-permute-start.7 = (bf16[1,2,360,192]{2,3,1,0:T(8,128)(2,1)}, bf16[1,2,360,192]{2,3,1,0:T(8,128)(2,1)S(1)}, u32[]{:S(2)}, u32[]{:S(2)}) collective-permute-start(bf16[1,2,360,192]{2,3,1,0:T(8,128)(2,1)} %slice_bitcast_fusion.26), channel_id=1, source_target_pairs={{1,0},{2,1},{3,2},{4,3},{5,4},{6,5},{7,6},{9,8},{10,9},{11,10},{12... | collective-permute-start | bytes 829448 | tf_op jit(solution)/shard_map/ppermute | solution.py:22
  265.8 235.3 %all-reduce.7.cloned.1.call-start = ((), (), s32[]{:S(2)}) async-start(), calls=%async_computation.1 | async-start | bytes 2359296 | tf_op jit(solution)/shard_map/psum | solution.py:104
  276.2 3.5 copy-start.5
  301.0 13.1 %copy-start.18 = (bf16[3,3,192,192]{2,3,1,0:T(8,128)(2,1)S(1)}, bf16[3,3,192,192]{2,3,1,0:T(8,128)(2,1)}, u32[]{:S(2)}) copy-start(bf16[3,3,192,192]{2,3,1,0:T(8,128)(2,1)} %copy-done.17) | copy-start | bytes 1990660
  329.2 115.6 %copy-start.4 = (bf16[1,16,360,192]{3,1,2,0:T(8,128)(2,1)S(1)}, bf16[1,16,360,192]{3,1,2,0:T(8,128)(2,1)}, u32[]{:S(2)}) copy-start(bf16[1,16,360,192]{3,1,2,0:T(8,128)(2,1)} %copy.60) | copy-start | bytes 6635524
  (10 other events, 14.9 us)
Sparse Core Ops, SparseCore 0:
  265.9 174.8 all-reduce.8
  444.9 56.1 all-reduce.6
